TPU v7x, 32 devices: a whole 2x2x4 slice. The times are simulated.
32 devices in a mesh: grp: 4 (over y, x), shard: 8 (over z, core).
Axes of the slice: x: 2, y: 2, z: 4, core: 2. Of those that a mesh axis runs over, the one named last changes fastest.
Arguments:
- partials: bfloat16 [4, 1536, 2, 4096], P('grp', 'shard'), may hold values from -225 to 225
- weights: float32 [1536, 2, 4096], P('shard'), may hold values from -4 to 4
- subspace: bfloat16 [1536, 2, 256], P('shard'), may hold values from -6 to 6
- moment_one: float32 [4096, 2, 256], P('shard'), may hold values from -2 to 2
- moment_two: float32 [4096, 2, 256], P('shard'), may hold values from 0.001 to 0.1
Outputs:
- new_weights: float32 [1536, 2, 4096], P('shard')
- new_moment_one: float32 [4096, 2, 256], P('shard')
- new_moment_two: float32 [4096, 2, 256], P('shard')
- new_subspace: bfloat16 [1536, 2, 256], P('shard')
All inputs are finite; a program needn't handle non-finite values.
Results may differ from a plain program's by a relative error of at most 0.01.
Values may be sent and summed in bfloat16 or wider, within the bound.
No kernel may reach another device: no remote copies, remote signals or barrier semaphores. Data moves between devices by JAX's collectives and lax.ppermute only.
A program may use at most 128 MiB of HBM per device.

v0:
```python
import math
import jax
import jax.numpy as jnp
from jax import lax
from jax.sharding import PartitionSpec as P

D = 1536
first_fix = 1.0 - 0.9**10
second_fix = 1.0 - 0.999**10


def per_device(partials, weights, subspace, moment_one, moment_two):
    gradient = lax.psum(partials[0].astype(jnp.float32).astype(jnp.bfloat16), "grp")
    inv_root = 1.0 / math.sqrt(D)
    column_block = gradient
    projected = lax.psum_scatter(
        jnp.einsum("dmf,dmk->fmk", column_block, subspace, preferred_element_type=jnp.float32)
        * inv_root,
        "shard",
        scatter_dimension=0,
        tiled=True,
    )
    new_moment_one = 0.9 * moment_one + 0.1 * projected
    new_moment_two = 0.999 * moment_two + 0.001 * projected * projected
    direction = (
        new_moment_one / first_fix / (jnp.sqrt(new_moment_two / second_fix) + 1e-08)
    ).astype(jnp.bfloat16)
    projected_half = projected.astype(jnp.bfloat16)
    update = jnp.einsum(
        "dmk,fmk->dmf",
        subspace,
        lax.all_gather(direction, "shard", axis=0, tiled=True),
        preferred_element_type=jnp.float32,
    )
    increment = update
    column_block = gradient
    spanned = jnp.einsum(
        "dmf,fmk->dmk",
        column_block,
        lax.all_gather(projected_half, "shard", axis=0, tiled=True),
        preferred_element_type=jnp.float32,
    )
    increment, spanned = (increment, spanned)
    new_weights = weights - increment * inv_root
    local_gram = jnp.einsum("dmk,dml->mkl", spanned, spanned, precision=lax.Precision.HIGHEST)
    gram_matrix = lax.psum(local_gram, "shard")
    normalizer = 1.7 / jnp.sqrt(jnp.sqrt(jnp.sum(gram_matrix * gram_matrix, axis=(1, 2))) + 1e-06)
    oriented = spanned * normalizer[None, :, None]
    own_gram = jnp.einsum("dmk,dml->mkl", oriented, oriented, precision=lax.Precision.HIGHEST)
    ortho_gram = lax.psum(own_gram, "shard")
    polished = 1.5 * oriented - 0.5 * jnp.einsum(
        "dmk,mkl->dml", oriented, ortho_gram, precision=lax.Precision.HIGHEST
    )
    new_subspace = (math.sqrt(D) * polished).astype(jnp.bfloat16)
    return (new_weights, new_moment_one, new_moment_two, new_subspace)


def solution(mesh):
    return jax.shard_map(
        per_device,
        mesh=mesh,
        in_specs=(
            P("grp", "shard", None, None),
            P("shard", None, None),
            P("shard", None, None),
            P("shard", None, None),
            P("shard", None, None),
        ),
        out_specs=(
            P("shard", None, None),
            P("shard", None, None),
            P("shard", None, None),
            P("shard", None, None),
        ),
        check_vma=False,
    )
```

profile of v0, /device:TPU:0, one launch (start us, length us, event | category | flops | bytes accessed | tf_op | source)
XLA Modules:
  0.0 424.1 jit_solution(8756850632732030668)
XLA Ops:
  7.2 5.7 %copy.29 = bf16[1,192,2,4096]{3,1,2,0:T(8,128)(2,1)} copy(bf16[1,192,2,4096]{3,2,1,0:T(2,128)(2,1)} %param.5) | data formatting | bytes 6291456 | tf_op args[0]
  13.0 90.0 %all-reduce.4.cloned.1.call-done = bf16[192,2,4096]{2,0,1:T(8,128)(2,1)} async-done(((bf16[192,2,4096]{2,0,1:T(8,128)(2,1)}), bf16[192,2,4096]{2,0,1:T(8,128)(2,1)}) %all-reduce.4.cloned.1.call-update) | async-done | bytes 3145744 | tf_op jit(solution)/shard_map/psum | solution.py:13
  103.0 6.5 %multiply_bitcast_fusion = f32[4096,2,256]{0,2,1:T(8,128)} fusion(bf16[192,2,4096]{2,0,1:T(8,128)(2,1)} %all-reduce.4.cloned.1.call-done, bf16[192,2,256]{2,1,0:T(2,128)(2,1)S(1)} %copy-done.3), kind=kOutput, calls=%fused_computation | convolution fusion | flops 807403520 | bytes 11730944 | tf_op jit(solution)/shard_map/dmf,dmk->fmk/dot_general | solution.py:17
  109.6 1.1 copy-done.2
  110.7 1.6 copy.9
  112.3 2.4 copy.12
  114.7 84.6 %reduce-scatter.2.cloned.1.call-done = f32[512,2,256]{0,2,1:T(8,128)} async-done(((f32[4096,2,256]{0,2,1:T(8,128)}), f32[512,2,256]{0,2,1:T(8,128)}) %reduce-scatter.2.cloned.1.call-update) | async-done | bytes 1048592 | tf_op jit(solution)/shard_map/reduce_scatter | solution.py:16
  199.3 4.4 %divide_convert_fusion = (bf16[512,2,256]{0,2,1:T(8,128)(2,1)}, f32[512,2,256]{0,2,1:T(8,128)}, f32[512,2,256]{0,2,1:T(8,128)}, bf16[512,2,256]{0,2,1:T(8,128)(2,1)}) fusion(f32[512,2,256]{0,2,1:T(8,128)} %reduce-scatter.2.cloned.1.call-done, f32[512,2,256]{0,2,1:T(8,128)} %copy.9, f32[512,2,256]{0,2,1:T(8,128)} %copy.12), kind=kLoop, calls=%fused_computation.11 | loop fusion | flops 3407872 | bytes 6291456 | tf_op jit(solution)/shard_map/convert_element_type | solution.py:27
  203.7 0.0 all-reduce.6.cloned.1.call-start
  203.8 45.6 %all-gather.5.cloned.1.call-done = bf16[4096,2,256]{0,2,1:T(8,128)(2,1)} async-done(((bf16[512,2,256]{0,2,1:T(8,128)(2,1)}), bf16[4096,2,256]{0,2,1:T(8,128)(2,1)}) %all-gather.5.cloned.1.call-update) | async-done | bytes 4194320 | tf_op jit(solution)/shard_map/all_gather | solution.py:40
  249.4 3.7 convolution_bitcast_fusion
  253.1 1.9 fusion.13
  255.1 0.5 all-gather.3.cloned.1.call-update
  255.7 2.4 copy.18
  258.1 1.3 copy.19
  259.4 50.6 %all-reduce.6.cloned.1.call-done = f32[2,256,256]{2,1,0:T(8,128)} async-done(((f32[2,256,256]{2,1,0:T(8,128)}), f32[2,256,256]{2,1,0:T(8,128)}) %all-reduce.6.cloned.1.call-update) | async-done | bytes 524304 | tf_op jit(solution)/shard_map/psum | solution.py:46
  310.1 1.2 multiply_reduce_fusion
  311.3 2.0 fusion.5
  313.3 44.4 %all-gather.3.cloned.1.call-done = bf16[4096,2,256]{0,2,1:T(8,128)(2,1)} async-done(((bf16[512,2,256]{0,2,1:T(8,128)(2,1)}), bf16[4096,2,256]{0,2,1:T(8,128)(2,1)}) %all-gather.3.cloned.1.call-update) | async-done | bytes 4194320 | tf_op jit(solution)/shard_map/all_gather | solution.py:32
  357.7 8.7 %bitcast_subtract_fusion = f32[192,2,4096]{2,0,1:T(8,128)S(1)} fusion(f32[192,2,4096]{2,1,0:T(2,128)} %param.6, bf16[4096,2,256]{0,2,1:T(8,128)(2,1)} %all-gather.3.cloned.1.call-done, bf16[192,2,256]{2,1,0:T(2,128)(2,1)} %param.7), kind=kOutput, calls=%fused_computation.1 | convolution fusion | flops 808452096 | bytes 16973824 | tf_op jit(solution)/shard_map/dmk,fmk->dmf/dot_general | solution.py:29
  366.4 7.6 %copy.17 = f32[192,2,4096]{2,1,0:T(2,128)} copy(f32[192,2,4096]{2,0,1:T(8,128)S(1)} %bitcast_subtract_fusion) | data formatting | bytes 12582912
  374.0 40.8 %all-reduce.8.cloned.1.call-done = f32[2,256,256]{2,1,0:T(8,128)} async-done(((f32[2,256,256]{2,1,0:T(8,128)}), f32[2,256,256]{2,1,0:T(8,128)}) %all-reduce.8.cloned.1.call-update) | async-done | bytes 524304 | tf_op jit(solution)/shard_map/psum | solution.py:50
  414.8 1.6 fusion.3
  416.4 0.9 copy.20
  (18 shorter events, 0.3 us)
Async XLA Ops:
  7.2 95.8 %copy-start.3 = (bf16[192,2,256]{2,1,0:T(2,128)(2,1)S(1)}, bf16[192,2,256]{2,1,0:T(2,128)(2,1)}, u32[]{:S(2)}) copy-start(bf16[192,2,256]{2,1,0:T(2,128)(2,1)} %param.7) | copy-start | bytes 589828
  7.2 95.8 %all-reduce.4.cloned.1.call-start = ((), (), s32[]{:S(2)}) async-start(), calls=%async_computation.1 | async-start | bytes 6291456 | tf_op jit(solution)/shard_map/psum | solution.py:13
  12.9 186.4 %reduce-scatter.2.cloned.1.call-start = ((), (), s32[]{:S(2)}) async-start(), calls=%async_computation.2 | async-start | bytes 9437184 | tf_op jit(solution)/shard_map/reduce_scatter | solution.py:16
  109.5 1.2 copy-start.2
  109.5 139.8 %all-gather.5.cloned.1.call-start = ((), (), s32[]{:S(2)}) async-start(), calls=%async_computation.4 | async-start | bytes 4718592 | tf_op jit(solution)/shard_map/all_gather | solution.py:40
  112.3 137.1 %copy-start = (bf16[192,2,4096]{2,0,1:T(8,128)(2,1)S(1)}, bf16[192,2,4096]{2,0,1:T(8,128)(2,1)}, u32[]{:S(2)}) copy-start(bf16[192,2,4096]{2,0,1:T(8,128)(2,1)} %all-reduce.4.cloned.1.call-done) | copy-start | bytes 9437188
  203.7 106.3 %all-reduce.6.cloned.1.call-start = ((), (), s32[]{:S(2)}) async-start(), calls=%async_computation.5 | async-start | bytes 1048576 | tf_op jit(solution)/shard_map/psum | solution.py:46
  253.1 5.0 %copy-start.1 = (f32[512,2,256]{0,2,1:T(8,128)S(1)}, f32[512,2,256]{0,2,1:T(8,128)}, u32[]{:S(2)}) copy-start(f32[512,2,256]{0,2,1:T(8,128)} %get-tuple-element.10) | copy-start | bytes 3145732
  255.1 102.6 %all-gather.3.cloned.1.call-start = ((), (), s32[]{:S(2)}) async-start(), calls=%async_computation.3 | async-start | bytes 4718592 | tf_op jit(solution)/shard_map/all_gather | solution.py:32
  255.7 159.1 %all-reduce.8.cloned.1.call-start = ((), (), s32[]{:S(2)}) async-start(), calls=%async_computation.6 | async-start | bytes 1048576 | tf_op jit(solution)/shard_map/psum | solution.py:50
Sparse Core Ops, SparseCore 0:
  13.1 89.8 all-reduce.3
  109.7 89.5 reduce-scatter.1
  203.8 45.5 all-gather.4
  255.2 54.8 all-reduce.5
  311.5 46.1 all-gather.2
  359.9 54.8 all-reduce.7
where the time goes:
time: 424 us
  waiting for transfers between devices  357 us (84%)
  matrix products  24.5 us (6%)
  local copies, waits for them, and re-layouts  23 us (5%)
  between operations  14.2 us (3%)
  other arithmetic  5.61 us (1%)
    psum x1, waiting for transfers between devices, per_device(): lax.psum(partials[0].astype(jnp.float32).astype(jnp.bfloat16), 'grp')  90 us
    reduce_scatter x1, waiting for transfers between devices, per_device(): lax.psum_scatter(jnp.einsum('dmf,dmk->fmk', column_block, subspace, prefe...  84.6 us
    psum x1, waiting for transfers between devices, per_device(): gram_matrix = lax.psum(local_gram, 'shard')  50.6 us
    all_gather x1, waiting for transfers between devices, per_device(): lax.all_gather(projected_half, 'shard', axis=0, tiled=True)  45.6 us
    all_gather x1, waiting for transfers between devices, per_device(): lax.all_gather(direction, 'shard', axis=0, tiled=True)  44.4 us
    psum x1, waiting for transfers between devices, per_device(): ortho_gram = lax.psum(own_gram, 'shard')  40.8 us
    unnamed x15, local copies, waits for them, and re-layouts  23 us
    dot_general x1, matrix products, per_device(): jnp.einsum('dmk,fmk->dmf', subspace, lax.all_gather(direction, 'shard', a...  8.71 us
  transfers between devices with their start and end apart: 6, of which 6 were waited for; matrix products, arithmetic and copies ran while one was open for 6% of the time, Pallas kernels for 0%

commit v1 on v0

--- a/solution.py
+++ b/solution.py
@@ -7,6 +7,40 @@
 D = 1536
 first_fix = 1.0 - 0.9**10
 second_fix = 1.0 - 0.999**10
+
+
+def _start_bars(own_rows, which_dim):
+    reply = list(own_rows.shape[1:])
+    reply[which_dim] *= own_rows.shape[0]
+    z2 = jnp.moveaxis(own_rows, 0, which_dim).reshape(reply)
+    return z2
+
+
+def return_all_view(array_dim, field, row_axis):
+    kept_rows = []
+    n_blocks = lax.axis_size(row_axis)
+    for m in range(n_blocks):
+        kept_rows.append((m, (m + 1) % n_blocks))
+    samples = []
+    for p, hop_no in kept_rows:
+        samples.append((hop_no, p))
+    outcome_arr, b_now = ([], [])
+    for to_i in range(n_blocks - 1):
+        if to_i % 2 == 0:
+            outcome_arr.append(
+                lax.ppermute(
+                    outcome_arr[-1] if outcome_arr else field, axis_name=row_axis, perm=kept_rows
+                )
+            )
+        else:
+            extra = lax.ppermute(b_now[-1] if b_now else field, axis_name=row_axis, perm=samples)
+            b_now.append(extra)
+    p_next = jnp.stack([*outcome_arr[::-1], field, *b_now])
+    r_now = lax.axis_index(row_axis)
+    z_new = r_now - len(outcome_arr)
+    p_next = p_next[(jnp.arange(n_blocks) - z_new) % n_blocks]
+    w1 = _start_bars(p_next, array_dim)
+    return w1
 
 
 def per_device(partials, weights, subspace, moment_one, moment_two):
@@ -29,7 +63,7 @@
     update = jnp.einsum(
         "dmk,fmk->dmf",
         subspace,
-        lax.all_gather(direction, "shard", axis=0, tiled=True),
+        return_all_view(0, direction, "shard"),
         preferred_element_type=jnp.float32,
     )
     increment = update

time: 424 us -> 423 us (level)
  waiting for transfers between devices: 357 us -> 320 us
  local copies, waits for them, and re-layouts: 23 us -> 47.9 us
  starting transfers between devices: 0.24 us -> 10.9 us
    ppermute x0 -> x7, waiting for transfers between devices: none -> 57.2 us  [the longest x4 57.2 us: return_all_view(): lax.ppermute(outcome_arr[-1] if outcome_arr else field, axis_name=row_axi...]
    all_gather x1, waiting for transfers between devices: 45.6 us -> 0.01 us  [per_device(): lax.all_gather(projected_half, 'shard', axis=0, tiled=True)]
    all_gather x1 -> x0, waiting for transfers between devices: 44.4 us -> none  [per_device(): lax.all_gather(direction, 'shard', axis=0, tiled=True)]
    unnamed x15 -> x26, local copies, waits for them, and re-layouts: 23 us -> 34.9 us
    gather x0 -> x2, local copies, waits for them, and re-layouts: none -> 11.1 us  [return_all_view(): p_next = p_next[(jnp.arange(n_blocks) - z_new) % n_blocks]]
    ppermute x0 -> x7, starting transfers between devices: none -> 10.7 us  [the longest x3 10.6 us: return_all_view(): lax.ppermute(b_now[-1] if b_now else field, axis_name=row_axis, perm=samp...]
  transfers between devices with their start and end apart: 6 -> 12, of which waited for: 6 -> 8; matrix products, arithmetic and copies ran while one was open for 6% -> 13% of each run, Pallas kernels for 0% -> 0%
where the time goes in v1:
time: 423 us; the launch traced here: 422 us
  waiting for transfers between devices  320 us (76%)
  local copies, waits for them, and re-layouts  47.9 us (11%)
  matrix products  24.4 us (6%)
  between operations  13.9 us (3%)
  starting transfers between devices  10.9 us (3%)
  other arithmetic  4.86 us (1%)
    psum x1, waiting for transfers between devices, per_device(): lax.psum(partials[0].astype(jnp.float32).astype(jnp.bfloat16), 'grp')  90 us
    reduce_scatter x1, waiting for transfers between devices, per_device(): lax.psum_scatter(jnp.einsum('dmf,dmk->fmk', column_block, subspace, prefe...  86.3 us
    ppermute x4, waiting for transfers between devices, return_all_view(): lax.ppermute(outcome_arr[-1] if outcome_arr else field, axis_name=row_axi...  57.2 us
    psum x1, waiting for transfers between devices, per_device(): gram_matrix = lax.psum(local_gram, 'shard')  47.2 us
    psum x1, waiting for transfers between devices, per_device(): ortho_gram = lax.psum(own_gram, 'shard')  39.1 us
    unnamed x26, local copies, waits for them, and re-layouts  34.9 us
    gather x2, local copies, waits for them, and re-layouts, return_all_view(): p_next = p_next[(jnp.arange(n_blocks) - z_new) % n_blocks]  11.1 us
    ppermute x3, starting transfers between devices, return_all_view(): lax.ppermute(b_now[-1] if b_now else field, axis_name=row_axis, perm=samp...  10.6 us
  transfers between devices with their start and end apart: 12, of which 8 were waited for; matrix products, arithmetic and copies ran while one was open for 13% of the time, Pallas kernels for 0%

profile of v1, /device:TPU:0, one launch (start us, length us, event | category | flops | bytes accessed | tf_op | source)
XLA Modules:
  0.0 421.7 jit_solution(9758437922620471443)
XLA Ops:
  7.2 5.7 %copy.39 = bf16[1,192,2,4096]{3,1,2,0:T(8,128)(2,1)} copy(bf16[1,192,2,4096]{3,2,1,0:T(2,128)(2,1)} %param.5) | data formatting | bytes 6291456 | tf_op args[0]
  13.0 90.0 %all-reduce.4.cloned.1.call-done = bf16[192,2,4096]{2,0,1:T(8,128)(2,1)} async-done(((bf16[192,2,4096]{2,0,1:T(8,128)(2,1)}), bf16[192,2,4096]{2,0,1:T(8,128)(2,1)}) %all-reduce.4.cloned.1.call-update) | async-done | bytes 3145744 | tf_op jit(solution)/shard_map/psum | solution.py:47
  103.0 6.5 %multiply_bitcast_fusion = f32[4096,2,256]{0,2,1:T(8,128)} fusion(bf16[192,2,4096]{2,0,1:T(8,128)(2,1)} %all-reduce.4.cloned.1.call-done, bf16[192,2,256]{2,1,0:T(2,128)(2,1)S(1)} %copy-done.3), kind=kOutput, calls=%fused_computation.1 | convolution fusion | flops 807403520 | bytes 11730944 | tf_op jit(solution)/shard_map/dmf,dmk->fmk/dot_general | solution.py:51
  113.0 86.3 %reduce-scatter.2.cloned.1.call-done = f32[512,2,256]{0,2,1:T(8,128)} async-done(((f32[4096,2,256]{0,2,1:T(8,128)}), f32[512,2,256]{0,2,1:T(8,128)}) %reduce-scatter.2.cloned.1.call-update) | async-done | bytes 1048592 | tf_op jit(solution)/shard_map/reduce_scatter | solution.py:50
  199.3 3.6 divide_convert_fusion
  203.0 10.8 %collective-permute-done = bf16[512,2,256]{0,2,1:T(8,128)(2,1)S(1)} collective-permute-done((bf16[512,2,256]{0,2,1:T(8,128)(2,1)}, bf16[512,2,256]{0,2,1:T(8,128)(2,1)S(1)}, u32[]{:S(2)}, u32[]{:S(2)}) %collective-permute-start) | collective-permute-done | bytes 524320 | tf_op jit(solution)/shard_map/ppermute | solution.py:31
  214.6 3.5 collective-permute-start.4
  218.2 22.8 %collective-permute-done.1 = bf16[512,2,256]{0,2,1:T(8,128)(2,1)S(1)} collective-permute-done((bf16[512,2,256]{0,2,1:T(8,128)(2,1)S(1)}, bf16[512,2,256]{0,2,1:T(8,128)(2,1)S(1)}, u32[]{:S(2)}, u32[]{:S(2)}) %collective-permute-start.1) | collective-permute-done | bytes 524320 | tf_op jit(solution)/shard_map/ppermute | solution.py:31
  241.8 3.5 collective-permute-start.5
  245.4 20.0 %collective-permute-done.2 = bf16[512,2,256]{0,2,1:T(8,128)(2,1)} collective-permute-done((bf16[512,2,256]{0,2,1:T(8,128)(2,1)S(1)}, bf16[512,2,256]{0,2,1:T(8,128)(2,1)}, u32[]{:S(2)}, u32[]{:S(2)}) %collective-permute-start.2) | collective-permute-done | bytes 524320 | tf_op jit(solution)/shard_map/ppermute | solution.py:31
  266.7 2.4 copy.30
  269.1 3.5 collective-permute-start.6
  272.6 3.6 collective-permute-done.3
  286.4 3.7 convolution_bitcast_fusion
  290.1 1.9 fusion.15
  292.1 1.9 bitcast_dynamic-update-slice_fusion.1
  293.9 1.9 bitcast_dynamic-update-slice_fusion
  295.8 4.9 %gather_fusion = bf16[8,512,2,256]{1,3,2,0:T(8,128)(2,1)} fusion(bf16[8,512,2,256]{1,3,2,0:T(8,128)(2,1)} %bitcast_dynamic-update-slice_fusion, s32[1024]{0:T(1024)S(1)} %pad_clamp_fusion), kind=kCustom, calls=%fused_computation | custom fusion | bytes 8388640 | tf_op jit(solution)/shard_map/gather | solution.py:41
  300.8 6.2 %copy.24 = bf16[8,512,2,256]{3,1,0,2:T(8,128)(2,1)} copy(bf16[8,512,2,256]{1,3,2,0:T(8,128)(2,1)} %gather_fusion) | data formatting | bytes 8388608 | tf_op jit(solution)/shard_map/gather | solution.py:41
  307.0 47.2 %all-reduce.6.cloned.1.call-done = f32[2,256,256]{2,1,0:T(8,128)} async-done(((f32[2,256,256]{2,1,0:T(8,128)}), f32[2,256,256]{2,1,0:T(8,128)}) %all-reduce.6.cloned.1.call-update) | async-done | bytes 524304 | tf_op jit(solution)/shard_map/psum | solution.py:80
  355.4 1.9 fusion.5
  357.3 8.7 %bitcast_subtract_fusion = f32[192,2,4096]{2,0,1:T(8,128)S(1)} fusion(f32[192,2,4096]{2,1,0:T(2,128)} %param.6, bf16[4096,2,256]{2,0,1:T(8,128)(2,1)} %bitcast.43, bf16[192,2,256]{2,1,0:T(2,128)(2,1)} %param.7), kind=kOutput, calls=%fused_computation.2 | convolution fusion | flops 808452096 | bytes 16973824 | tf_op jit(solution)/shard_map/dmk,fmk->dmf/dot_general | solution.py:63
  366.0 7.6 %copy.28 = f32[192,2,4096]{2,1,0:T(2,128)} copy(f32[192,2,4096]{2,0,1:T(8,128)S(1)} %bitcast_subtract_fusion) | data formatting | bytes 12582912
  373.6 39.1 %all-reduce.8.cloned.1.call-done = f32[2,256,256]{2,1,0:T(8,128)} async-done(((f32[2,256,256]{2,1,0:T(8,128)}), f32[2,256,256]{2,1,0:T(8,128)}) %all-reduce.8.cloned.1.call-update) | async-done | bytes 524304 | tf_op jit(solution)/shard_map/psum | solution.py:84
  (45 shorter events, 20.6 us)
Async XLA Ops:
  7.2 95.8 %copy-start.3 = (bf16[192,2,256]{2,1,0:T(2,128)(2,1)S(1)}, bf16[192,2,256]{2,1,0:T(2,128)(2,1)}, u32[]{:S(2)}) copy-start(bf16[192,2,256]{2,1,0:T(2,128)(2,1)} %param.7) | copy-start | bytes 589828
  7.2 95.8 %all-reduce.4.cloned.1.call-start = ((), (), s32[]{:S(2)}) async-start(), calls=%async_computation.1 | async-start | bytes 6291456 | tf_op jit(solution)/shard_map/psum | solution.py:47
  12.9 186.3 %reduce-scatter.2.cloned.1.call-start = ((), (), s32[]{:S(2)}) async-start(), calls=%async_computation.2 | async-start | bytes 9437184 | tf_op jit(solution)/shard_map/reduce_scatter | solution.py:50
  109.5 1.2 copy-start.2
  109.5 176.9 %all-gather.2.cloned.1.call-start = ((), (), s32[]{:S(2)}) async-start(), calls=%async_computation.3 | async-start | bytes 4718592 | tf_op jit(solution)/shard_map/all_gather | solution.py:74
  202.9 151.2 %all-reduce.6.cloned.1.call-start = ((), (), s32[]{:S(2)}) async-start(), calls=%async_computation.4 | async-start | bytes 1048576 | tf_op jit(solution)/shard_map/psum | solution.py:80
  203.0 10.8 %collective-permute-start = (bf16[512,2,256]{0,2,1:T(8,128)(2,1)}, bf16[512,2,256]{0,2,1:T(8,128)(2,1)S(1)}, u32[]{:S(2)}, u32[]{:S(2)}) collective-permute-start(bf16[512,2,256]{0,2,1:T(8,128)(2,1)} %get-tuple-element.12), channel_id=1, source_target_pairs={{0,1},{1,2},{2,3},{3,4},{4,5},{5,6},{6,7},{7,0},{8,9},{9,10},{10,1... | collective-permute-start | bytes 1572872 | tf_op jit(solution)/shard_map/ppermute | solution.py:31
  213.8 0.8 copy-start.4
  214.6 26.4 %collective-permute-start.1 = (bf16[512,2,256]{0,2,1:T(8,128)(2,1)S(1)}, bf16[512,2,256]{0,2,1:T(8,128)(2,1)S(1)}, u32[]{:S(2)}, u32[]{:S(2)}) collective-permute-start(bf16[512,2,256]{0,2,1:T(8,128)(2,1)S(1)} %collective-permute-done), channel_id=1, source_target_pairs={{0,1},{1,2},{2,3},{3,4},{4,5},{5,6},{6,7},{7,0},{8,9},{9,10},{10,1... | collective-permute-start | bytes 1572872 | tf_op jit(solution)/shard_map/ppermute | solution.py:31
  214.6 27.2 %collective-permute-start.4 = (bf16[512,2,256]{0,2,1:T(8,128)(2,1)}, bf16[512,2,256]{0,2,1:T(8,128)(2,1)}, u32[]{:S(2)}, u32[]{:S(2)}) collective-permute-start(bf16[512,2,256]{0,2,1:T(8,128)(2,1)} %get-tuple-element.12), channel_id=1, source_target_pairs={{1,0},{2,1},{3,2},{4,3},{5,4},{6,5},{7,6},{0,7},{9,8},{10,9},{11,1... | collective-permute-start | bytes 1572872 | tf_op jit(solution)/shard_map/ppermute | solution.py:36
  241.0 0.8 copy-start.5
  241.8 23.5 %collective-permute-start.2 = (bf16[512,2,256]{0,2,1:T(8,128)(2,1)S(1)}, bf16[512,2,256]{0,2,1:T(8,128)(2,1)}, u32[]{:S(2)}, u32[]{:S(2)}) collective-permute-start(bf16[512,2,256]{0,2,1:T(8,128)(2,1)S(1)} %collective-permute-done.1), channel_id=1, source_target_pairs={{0,1},{1,2},{2,3},{3,4},{4,5},{5,6},{6,7},{7,0},{8,9},{9,10},{10,1... | collective-permute-start | bytes 1572872 | tf_op jit(solution)/shard_map/ppermute | solution.py:31
  241.8 27.3 %collective-permute-start.5 = (bf16[512,2,256]{0,2,1:T(8,128)(2,1)}, bf16[512,2,256]{0,2,1:T(8,128)(2,1)}, u32[]{:S(2)}, u32[]{:S(2)}) collective-permute-start(bf16[512,2,256]{0,2,1:T(8,128)(2,1)} %collective-permute-done.4), channel_id=1, source_target_pairs={{1,0},{2,1},{3,2},{4,3},{5,4},{6,5},{7,6},{0,7},{9,8},{10,9},{11,1... | collective-permute-start | bytes 1572872 | tf_op jit(solution)/shard_map/ppermute | solution.py:36
  265.4 10.9 %collective-permute-start.3 = (bf16[512,2,256]{0,2,1:T(8,128)(2,1)}, bf16[512,2,256]{0,2,1:T(8,128)(2,1)}, u32[]{:S(2)}, u32[]{:S(2)}) collective-permute-start(bf16[512,2,256]{0,2,1:T(8,128)(2,1)} %collective-permute-done.2), channel_id=1, source_target_pairs={{0,1},{1,2},{2,3},{3,4},{4,5},{5,6},{6,7},{7,0},{8,9},{9,10},{10,1... | collective-permute-start | bytes 1572872 | tf_op jit(solution)/shard_map/ppermute | solution.py:31
  266.7 19.7 %copy-start = (bf16[192,2,4096]{2,0,1:T(8,128)(2,1)S(1)}, bf16[192,2,4096]{2,0,1:T(8,128)(2,1)}, u32[]{:S(2)}) copy-start(bf16[192,2,4096]{2,0,1:T(8,128)(2,1)} %all-reduce.4.cloned.1.call-done) | copy-start | bytes 9437188
  269.1 14.6 %copy-start.1 = (bf16[512,2,256]{0,2,1:T(8,128)(2,1)S(1)}, bf16[512,2,256]{0,2,1:T(8,128)(2,1)}, u32[]{:S(2)}) copy-start(bf16[512,2,256]{0,2,1:T(8,128)(2,1)} %get-tuple-element.12) | copy-start | bytes 1572868
  269.1 24.9 %collective-permute-start.6 = (bf16[512,2,256]{0,2,1:T(8,128)(2,1)}, bf16[512,2,256]{0,2,1:T(8,128)(2,1)}, u32[]{:S(2)}, u32[]{:S(2)}) collective-permute-start(bf16[512,2,256]{0,2,1:T(8,128)(2,1)} %collective-permute-done.5), channel_id=1, source_target_pairs={{1,0},{2,1},{3,2},{4,3},{5,4},{6,5},{7,6},{0,7},{9,8},{10,9},{11,1... | collective-permute-start | bytes 1572872 | tf_op jit(solution)/shard_map/ppermute | solution.py:36
  292.0 120.6 %all-reduce.8.cloned.1.call-start = ((), (), s32[]{:S(2)}) async-start(), calls=%async_computation.5 | async-start | bytes 1048576 | tf_op jit(solution)/shard_map/psum | solution.py:84
Sparse Core Ops, SparseCore 0:
  13.1 89.8 all-reduce.3
  109.7 89.5 reduce-scatter.1
  203.1 65.1 all-gather.1
  292.1 61.9 all-reduce.5
  357.5 55.1 all-reduce.7
